TPU v7x, 256 devices: a whole 4x4x8 slice. The times are simulated.
256 devices in a mesh: facet: 16 (over y, x_hi, core), bl: 16 (over z, x_lo).
Axes of the slice: x: 4 (x_hi: 2, x_lo: 2; x = x_hi * 2 + x_lo), y: 4, z: 8, core: 2. Of those that a mesh axis runs over, the one named last changes fastest.
Arguments:
- facet_model: bfloat16 [16, 1024, 1024], P('facet', 'bl'), may hold values from -0.005859375 to 0.005859375
- screens: bfloat16 [16, 256, 64, 128], P('facet', 'bl'), may hold values from 0.099609375 to 1.8984375
- observed: float32 [192, 64, 128], P('bl'), may hold values from -24 to 24
- offsets: int32 [192, 2], P('bl'), may hold values from 0 to 4032
- stations: int32 [192, 2], P('bl'), may hold values from 0 to 255
- counts: int32 [16], P('bl'), may hold values from 1 to 12, as said below
Outputs:
- residual_vis: float32 [192, 64, 128], P('bl')
- residual_image: float32 [16, 1024, 1024], P('facet', 'bl')
Inputs may be any that keep to these rules, and one draw needn't show every extreme that they name: `counts`: some baseline block has all 12 slots live.
All inputs are finite; a program needn't handle non-finite values.
Results may differ from a plain program's by a relative error of at most 0.0061.
Values may be sent and summed in bfloat16 or wider, within the bound.
No kernel may reach another device: no remote copies, remote signals or barrier semaphores. Data moves between devices by JAX's collectives and lax.ppermute only.
A program may use at most 64 MiB of HBM per device.

v0:
```python
import math
import jax
import jax.numpy as jnp
from jax import lax
from jax.sharding import PartitionSpec as P

FGRID = 4


def tables(offset_u, offset_v, facet_id, tile_width, facet_cells):
    grid_cells = FGRID * facet_cells
    corner_x = facet_id // FGRID * facet_cells
    corner_y = facet_id % FGRID * facet_cells
    pixel_index = jnp.arange(facet_cells, dtype=jnp.int32)
    cell_index = jnp.arange(tile_width, dtype=jnp.int32)
    phase_u = jnp.mod(
        (offset_u + cell_index)[:, None] * (corner_x + pixel_index)[None, :], grid_cells
    )
    phase_v = jnp.mod(
        (offset_v + cell_index)[:, None] * (corner_y + pixel_index)[None, :], grid_cells
    )
    angle_u = phase_u.astype(jnp.float32) * (2.0 * math.pi / grid_cells)
    angle_v = phase_v.astype(jnp.float32) * (2.0 * math.pi / grid_cells)
    tab_u = jnp.concatenate([jnp.cos(angle_u), -jnp.sin(angle_u)], axis=0).astype(jnp.bfloat16)
    table_vertical = jnp.concatenate([jnp.cos(angle_v), jnp.sin(angle_v)], axis=0).astype(
        jnp.bfloat16
    )
    return (tab_u, table_vertical)


def half_splits(value):
    half_width = value.shape[-1] // 2
    return (value[..., :half_width], value[..., half_width:])


def complex_times(left_re, left_im, right_re, right_im):
    return (left_re * right_re - left_im * right_im, left_re * right_im + left_im * right_re)


def times_conj(left_re, left_im, right_re, right_im):
    return (left_re * right_re + left_im * right_im, left_im * right_re - left_re * right_im)


def per_device(facet_model, screens, observed, offsets, stations, counts):
    tile_count = observed.shape[0]
    tile_width = observed.shape[1]
    facet_cells = facet_model.shape[2]
    bl_devices = lax.axis_size("bl")
    facet_id = lax.axis_index("facet")
    make_tables = jax.vmap(tables, in_axes=(0, 0, None, None, None))
    tab_u, table_vertical = make_tables(
        offsets[:, 0], offsets[:, 1], facet_id, tile_width, facet_cells
    )
    upper_portion = jnp.einsum(
        "tkn,np->tkp",
        tab_u,
        lax.all_gather(facet_model[0], "bl", axis=0, tiled=True),
        preferred_element_type=jnp.float32,
    ).astype(jnp.bfloat16)
    block_groups = jnp.einsum(
        "gsf,gmf->gsm", upper_portion, table_vertical, preferred_element_type=jnp.float32
    )
    real_part = (
        block_groups[:, :tile_width, :tile_width] + block_groups[:, tile_width:, tile_width:]
    )
    imag_part = (
        block_groups[:, tile_width:, :tile_width] - block_groups[:, :tile_width, tile_width:]
    )
    all_screens = lax.all_gather(screens[0], "bl", axis=0, tiled=True)
    first_station_gain = jnp.take(all_screens, stations[:, 0], axis=0).astype(jnp.float32)
    gain_q = jnp.take(all_screens, stations[:, 1], axis=0).astype(jnp.float32)
    p_re, p_im = half_splits(first_station_gain)
    q_re, q_im = half_splits(gain_q)
    y_re, y_im = complex_times(p_re, p_im, real_part, imag_part)
    x_re, x_im = times_conj(y_re, y_im, q_re, q_im)
    contribution = jnp.concatenate([x_re, x_im], axis=2)
    live_mask = (jnp.arange(tile_count, dtype=jnp.int32) < counts[0])[:, None, None]
    predicted = lax.psum(contribution, "facet")
    residual = jnp.where(live_mask, observed - predicted, jnp.zeros_like(observed))
    r_re, r_im = half_splits(residual)
    z_re, z_im = times_conj(r_re, r_im, p_re, p_im)
    w_re, w_im = complex_times(z_re, z_im, q_re, q_im)
    w_re = w_re.astype(jnp.bfloat16)
    w_im = w_im.astype(jnp.bfloat16)
    stacked = jnp.concatenate(
        [jnp.concatenate([w_re, -w_im], axis=2), jnp.concatenate([w_im, w_re], axis=2)], axis=1
    )
    q_two = jnp.einsum(
        "tuk,tky->tuy", stacked, table_vertical, preferred_element_type=jnp.float32
    ).astype(jnp.bfloat16)
    image_scale = 1.0 / (32.0 * tile_width * math.sqrt(tile_count * bl_devices))
    row_count = facet_cells // bl_devices
    whole_image = jnp.einsum("tkx,tky->xy", tab_u, q_two, preferred_element_type=jnp.float32)
    summed = lax.psum(whole_image, "bl")
    own_rows = lax.dynamic_slice_in_dim(summed, lax.axis_index("bl") * row_count, row_count, 0)
    residual_image = (own_rows * image_scale)[None]
    return (residual, residual_image)


def solution(mesh):
    in_specs = (
        P("facet", "bl", None),
        P("facet", "bl", None, None),
        P("bl", None, None),
        P("bl", None),
        P("bl", None),
        P("bl"),
    )
    out_specs = (P("bl", None, None), P("facet", "bl", None))
    return jax.shard_map(
        per_device, mesh=mesh, in_specs=in_specs, out_specs=out_specs, check_vma=False
    )
```

profile of v0, /device:TPU:16, one launch (start us, length us, event | category | flops | bytes accessed | tf_op | source)
XLA Modules:
  0.0 557.0 jit_solution(6302353294279317188)
XLA Ops:
  7.2 0.0 all-gather.7.cloned.1.call-start
  7.2 0.7 all-gather.7.cloned.1.call-update
  7.9 0.0 all-gather.5.cloned.1.call-start
  7.9 0.7 all-gather.5.cloned.1.call-update
  8.6 0.0 all-reduce.3.cloned.1.call-start
  8.7 0.8 compare_and_fusion.1
  9.5 0.8 slice_bitcast_fusion.1
  10.3 0.1 iota_add_fusion
  10.4 14.1 %cosine_convert_fusion = (bf16[12,64,1024]{2,1,0:T(8,128)(2,1)S(1)}, bf16[12,64,1024]{2,1,0:T(8,128)(2,1)}) fusion(s32[1024]{0:T(1024)S(1)} %iota_add_fusion.2, s32[12,64]{1,0:T(8,128)S(1)} %get-tuple-element.24), kind=kLoop, calls=%fused_computation.23 | loop fusion | flops 12582912 | bytes 3152896 | tf_op jit(solution)/shard_map/convert
  24.4 14.2 %cosine_convert_fusion.1 = (bf16[12,64,1024]{2,1,0:T(8,128)(2,1)}, bf16[12,64,1024]{2,1,0:T(8,128)(2,1)}) fusion(s32[1024]{0:T(1024)S(1)} %iota_add_fusion.3, s32[12,64]{1,0:T(8,128)S(1)} %get-tuple-element.25), kind=kLoop, calls=%fused_computation.27 | loop fusion | flops 13369344 | bytes 3152896 | tf_op jit(solution)/shard_map/convert.2
  38.7 46.7 %all-gather.7.cloned.1.call-done = bf16[1,1024,1024]{2,1,0:T(8,128)(2,1)} async-done(((bf16[1,64,1024]{2,1,0:T(8,128)(2,1)}), bf16[1,1024,1024]{2,1,0:T(8,128)(2,1)}) %all-gather.7.cloned.1.call-update) | async-done | bytes 2097168 | tf_op jit(solution)/shard_map/all_gather | solution.py:57
  85.4 7.2 %fusion.8 = f32[12,128,128]{2,1,0:T(8,128)S(1)} fusion(bf16[12,64,1024]{2,1,0:T(8,128)(2,1)} %get-tuple-element.17, bf16[12,64,1024]{2,1,0:T(8,128)(2,1)S(1)} %get-tuple-element.16, bf16[1,1024,1024]{2,1,0:T(8,128)(2,1)} %all-gather.7.cloned.1.call-done, bf16[12,64,1024]{2,1,0:T(8,128)(2,1)} %get-tuple-element.15, bf16[12,64,1024]{2,1,0:T(8,128)(2,1)} %get-tuple-element.14), kind=kOutput, calls=%fused_computation.24 | convolution fusion | flops 3638034432 | bytes 9175040 | tf_op jit(solution)/shard_map/gsf,gmf->gsm/dot_general | solution.py:60
  92.6 92.0 %all-gather.5.cloned.1.call-done = bf16[1,256,64,128]{3,2,0,1:T(8,128)(2,1)} async-done(((bf16[1,16,64,128]{3,2,0,1:T(8,128)(2,1)}), bf16[1,256,64,128]{3,2,0,1:T(8,128)(2,1)}) %all-gather.5.cloned.1.call-update) | async-done | bytes 4194320 | tf_op jit(solution)/shard_map/all_gather | solution.py:69
  184.6 2.8 gather_fusion.1
  187.4 2.8 gather_fusion
  190.1 0.1 select_convert_fusion
  190.3 0.0 copy-start.1
  190.3 0.5 multiply_add_fusion.1
  190.8 0.2 multiply_subtract_fusion.1
  191.0 0.9 pad_maximum_fusion.11
  191.9 0.0 all-reduce.3.cloned.1.call-update
  191.9 0.2 all-reduce.5.cloned.1.call-start
  192.8 134.5 %all-reduce.3.cloned.1.call-done = f32[12,64,128]{2,1,0:T(8,128)} async-done(((f32[12,64,128]{2,1,0:T(8,128)}), f32[12,64,128]{2,1,0:T(8,128)}) %all-reduce.3.cloned.1.call-update) | async-done | bytes 393232 | tf_op jit(solution)/shard_map/psum | solution.py:78
  327.3 0.0 copy-done.1
  327.3 1.1 subtract_select_fusion
  328.4 0.0 copy-start
  328.4 0.4 fusion.39
  328.8 0.2 subtract_convert_fusion
  329.0 8.6 %fusion.12 = f32[1024,1024]{1,0:T(8,128)} fusion(bf16[12,64,1024]{2,1,0:T(8,128)(2,1)} %get-tuple-element.17, bf16[12,64,1024]{2,1,0:T(8,128)(2,1)S(1)} %get-tuple-element.16, bf16[12,64,1024]{2,1,0:T(8,128)(2,1)} %get-tuple-element.15, bf16[12,64,1024]{2,1,0:T(8,128)(2,1)} %get-tuple-element.14, bf16[12,64,64]{2,1,0:T(8,128)(2,1)S(1)} %subtract_convert_fusion, ...), kind=kOutput, calls=%fused_computation.29 | convolution fusion | flops 3639607296 | bytes 10780672 | tf_op jit(solution)/shard_map/tkx,tky->xy/dot_general | solution.py:93
  337.6 0.0 copy-done
  337.6 0.0 all-reduce.5.cloned.1.call-update
  337.7 211.1 %all-reduce.5.cloned.1.call-done = f32[1024,1024]{1,0:T(8,128)} async-done(((f32[1024,1024]{1,0:T(8,128)}), f32[1024,1024]{1,0:T(8,128)}) %all-reduce.5.cloned.1.call-update) | async-done | bytes 4194320 | tf_op jit(solution)/shard_map/psum | solution.py:94
  548.8 1.7 multiply_bitcast_fusion
  (5 shorter events, 0.0 us)
Async XLA Ops:
  7.2 78.2 %all-gather.7.cloned.1.call-start = ((), (), s32[]{:S(2)}) async-start(), calls=%async_computation.3 | async-start | bytes 2228224 | tf_op jit(solution)/shard_map/all_gather | solution.py:57
  7.9 176.7 %all-gather.5.cloned.1.call-start = ((), (), s32[]{:S(2)}) async-start(), calls=%async_computation.2 | async-start | bytes 4456448 | tf_op jit(solution)/shard_map/all_gather | solution.py:69
  8.6 318.6 %all-reduce.3.cloned.1.call-start = ((), (), s32[]{:S(2)}) async-start(), calls=%async_computation | async-start | bytes 786432 | tf_op jit(solution)/shard_map/psum | solution.py:78
  190.3 137.0 %copy-start.1 = (f32[12,64,128]{2,1,0:T(8,128)S(1)}, f32[12,64,128]{2,1,0:T(8,128)}, u32[]{:S(2)}) copy-start(f32[12,64,128]{2,1,0:T(8,128)} %param.10) | copy-start | bytes 1179652
  191.9 356.9 %all-reduce.5.cloned.1.call-start = ((), (), s32[]{:S(2)}) async-start(), calls=%async_computation.1 | async-start | bytes 8388608 | tf_op jit(solution)/shard_map/psum | solution.py:94
  328.4 9.2 %copy-start = (f32[12,64,128]{2,1,0:T(8,128)}, f32[12,64,128]{2,1,0:T(8,128)S(1)}, u32[]{:S(2)}) copy-start(f32[12,64,128]{2,1,0:T(8,128)S(1)} %subtract_select_fusion) | copy-start | bytes 1179652
Sparse Core Ops, SparseCore 0:
  9.8 75.5 all-gather.6
  87.2 97.3 all-gather.4
  192.0 135.2 all-reduce.2
  337.8 210.9 all-reduce.4
where the time goes:
time: 557 us
  waiting for transfers between devices  486 us (87%)
  other arithmetic  34.2 us (6%)
  matrix products  15.9 us (3%)
  between operations  14.6 us (3%)
  local copies, waits for them, and re-layouts  6.31 us (1%)
    psum x1, waiting for transfers between devices, per_device(): summed = lax.psum(whole_image, 'bl')  211 us
    psum x1, waiting for transfers between devices, per_device(): predicted = lax.psum(contribution, 'facet')  134 us
    all_gather x1, waiting for transfers between devices, per_device(): all_screens = lax.all_gather(screens[0], 'bl', axis=0, tiled=True)  92 us
    all_gather x1, waiting for transfers between devices, per_device(): lax.all_gather(facet_model[0], 'bl', axis=0, tiled=True)  46.7 us
    another operation x2, other arithmetic  28.3 us
  transfers between devices with their start and end apart: 4, of which 4 were waited for; matrix products, arithmetic and copies ran while one was open for 7% of the time, Pallas kernels for 0%

commit v1 on v0

--- a/solution.py
+++ b/solution.py
@@ -75,7 +75,7 @@
     x_re, x_im = times_conj(y_re, y_im, q_re, q_im)
     contribution = jnp.concatenate([x_re, x_im], axis=2)
     live_mask = (jnp.arange(tile_count, dtype=jnp.int32) < counts[0])[:, None, None]
-    predicted = lax.psum(contribution, "facet")
+    predicted = jnp.sum(lax.all_gather(contribution, "facet"), axis=0)
     residual = jnp.where(live_mask, observed - predicted, jnp.zeros_like(observed))
     r_re, r_im = half_splits(residual)
     z_re, z_im = times_conj(r_re, r_im, p_re, p_im)

time: 557 us -> 480 us (0.86)
  waiting for transfers between devices: 486 us -> 407 us
    psum x1 -> x0, waiting for transfers between devices: 134 us -> none  [per_device(): predicted = lax.psum(contribution, 'facet')]
    all_gather x0 -> x1, waiting for transfers between devices: none -> 66 us  [per_device(): predicted = jnp.sum(lax.all_gather(contribution, 'facet'), axis=0)]
    psum x1, waiting for transfers between devices: 211 us -> 200 us  [per_device(): summed = lax.psum(whole_image, 'bl')]
  transfers between devices with their start and end apart: 4 -> 4, of which waited for: 4 -> 4; matrix products, arithmetic and copies ran while one was open for 7% -> 8% of each run, Pallas kernels for 0% -> 0%
where the time goes in v1:
time: 480 us
  waiting for transfers between devices  407 us (85%)
  other arithmetic  36.6 us (8%)
  matrix products  15.9 us (3%)
  between operations  14.6 us (3%)
  local copies, waits for them, and re-layouts  6.31 us (1%)
    psum x1, waiting for transfers between devices, per_device(): summed = lax.psum(whole_image, 'bl')  200 us
    all_gather x1, waiting for transfers between devices, per_device(): all_screens = lax.all_gather(screens[0], 'bl', axis=0, tiled=True)  92 us
    all_gather x1, waiting for transfers between devices, per_device(): predicted = jnp.sum(lax.all_gather(contribution, 'facet'), axis=0)  66 us
    all_gather x1, waiting for transfers between devices, per_device(): lax.all_gather(facet_model[0], 'bl', axis=0, tiled=True)  46.7 us
    another operation x2, other arithmetic  28.3 us
  transfers between devices with their start and end apart: 4, of which 4 were waited for; matrix products, arithmetic and copies ran while one was open for 8% of the time, Pallas kernels for 0%

profile of v1, /device:TPU:16, one launch (start us, length us, event | category | flops | bytes accessed | tf_op | source)
XLA Modules:
  0.0 480.3 jit_solution(14527273502621721568)
XLA Ops:
  7.2 0.0 all-gather.9.cloned.1.call-start
  7.2 0.7 all-gather.9.cloned.1.call-update
  7.9 0.0 all-gather.7.cloned.1.call-start
  7.9 0.7 all-gather.7.cloned.1.call-update
  8.6 0.0 all-gather.11.cloned.1.call-start
  8.7 0.8 compare_and_fusion.1
  9.5 0.8 slice_bitcast_fusion.1
  10.3 0.1 iota_add_fusion
  10.4 14.1 %cosine_convert_fusion = (bf16[12,64,1024]{2,1,0:T(8,128)(2,1)S(1)}, bf16[12,64,1024]{2,1,0:T(8,128)(2,1)}) fusion(s32[1024]{0:T(1024)S(1)} %iota_add_fusion.2, s32[12,64]{1,0:T(8,128)S(1)} %get-tuple-element.24), kind=kLoop, calls=%fused_computation.23 | loop fusion | flops 12582912 | bytes 3152896 | tf_op jit(solution)/shard_map/convert
  24.4 14.2 %cosine_convert_fusion.1 = (bf16[12,64,1024]{2,1,0:T(8,128)(2,1)}, bf16[12,64,1024]{2,1,0:T(8,128)(2,1)}) fusion(s32[1024]{0:T(1024)S(1)} %iota_add_fusion.3, s32[12,64]{1,0:T(8,128)S(1)} %get-tuple-element.25), kind=kLoop, calls=%fused_computation.27 | loop fusion | flops 13369344 | bytes 3152896 | tf_op jit(solution)/shard_map/convert.2
  38.7 46.7 %all-gather.9.cloned.1.call-done = bf16[1,1024,1024]{2,1,0:T(8,128)(2,1)} async-done(((bf16[1,64,1024]{2,1,0:T(8,128)(2,1)}), bf16[1,1024,1024]{2,1,0:T(8,128)(2,1)}) %all-gather.9.cloned.1.call-update) | async-done | bytes 2097168 | tf_op jit(solution)/shard_map/all_gather | solution.py:57
  85.4 7.2 %fusion.8 = f32[12,128,128]{2,1,0:T(8,128)S(1)} fusion(bf16[12,64,1024]{2,1,0:T(8,128)(2,1)} %get-tuple-element.17, bf16[12,64,1024]{2,1,0:T(8,128)(2,1)S(1)} %get-tuple-element.16, bf16[1,1024,1024]{2,1,0:T(8,128)(2,1)} %all-gather.9.cloned.1.call-done, bf16[12,64,1024]{2,1,0:T(8,128)(2,1)} %get-tuple-element.15, bf16[12,64,1024]{2,1,0:T(8,128)(2,1)} %get-tuple-element.14), kind=kOutput, calls=%fused_computation.24 | convolution fusion | flops 3638034432 | bytes 9175040 | tf_op jit(solution)/shard_map/gsf,gmf->gsm/dot_general | solution.py:60
  92.6 92.0 %all-gather.7.cloned.1.call-done = bf16[1,256,64,128]{3,2,0,1:T(8,128)(2,1)} async-done(((bf16[1,16,64,128]{3,2,0,1:T(8,128)(2,1)}), bf16[1,256,64,128]{3,2,0,1:T(8,128)(2,1)}) %all-gather.7.cloned.1.call-update) | async-done | bytes 4194320 | tf_op jit(solution)/shard_map/all_gather | solution.py:69
  184.6 2.8 gather_fusion
  187.4 2.8 gather_fusion.1
  190.1 0.1 select_convert_fusion
  190.3 0.5 multiply_add_fusion.1
  190.8 0.2 multiply_subtract_fusion.1
  190.9 0.9 pad_maximum_fusion.11
  191.9 0.0 all-gather.11.cloned.1.call-update
  191.9 0.2 all-reduce.2.cloned.1.call-start
  192.8 66.0 %all-gather.11.cloned.1.call-done = f32[192,64,128]{2,1,0:T(8,128)} async-done(((f32[12,64,128]{2,1,0:T(8,128)}), f32[192,64,128]{2,1,0:T(8,128)}) %all-gather.11.cloned.1.call-update) | async-done | bytes 6291472 | tf_op jit(solution)/shard_map/all_gather | solution.py:78
  258.8 0.0 copy-start.1
  258.8 3.4 reduce_sum.9
  262.2 0.0 copy-done.1
  262.2 0.1 subtract_select_fusion
  262.3 0.0 copy-start
  262.3 0.4 fusion.39
  262.7 0.2 subtract_convert_fusion
  262.9 8.7 %fusion.12 = f32[1024,1024]{1,0:T(8,128)} fusion(bf16[12,64,1024]{2,1,0:T(8,128)(2,1)} %get-tuple-element.17, bf16[12,64,1024]{2,1,0:T(8,128)(2,1)S(1)} %get-tuple-element.16, bf16[12,64,1024]{2,1,0:T(8,128)(2,1)} %get-tuple-element.15, bf16[12,64,1024]{2,1,0:T(8,128)(2,1)} %get-tuple-element.14, bf16[12,64,64]{2,1,0:T(8,128)(2,1)S(1)} %subtract_convert_fusion, ...), kind=kOutput, calls=%fused_computation.29 | convolution fusion | flops 3639607296 | bytes 10780672 | tf_op jit(solution)/shard_map/tkx,tky->xy/dot_general | solution.py:93
  271.6 0.0 copy-done
  271.6 0.0 all-reduce.2.cloned.1.call-update
  271.6 200.5 %all-reduce.2.cloned.1.call-done = f32[1024,1024]{1,0:T(8,128)} async-done(((f32[1024,1024]{1,0:T(8,128)}), f32[1024,1024]{1,0:T(8,128)}) %all-reduce.2.cloned.1.call-update) | async-done | bytes 4194320 | tf_op jit(solution)/shard_map/psum | solution.py:94
  472.1 1.7 multiply_bitcast_fusion
  (5 shorter events, 0.0 us)
Async XLA Ops:
  7.2 78.2 %all-gather.9.cloned.1.call-start = ((), (), s32[]{:S(2)}) async-start(), calls=%async_computation.2 | async-start | bytes 2228224 | tf_op jit(solution)/shard_map/all_gather | solution.py:57
  7.9 176.7 %all-gather.7.cloned.1.call-start = ((), (), s32[]{:S(2)}) async-start(), calls=%async_computation.1 | async-start | bytes 4456448 | tf_op jit(solution)/shard_map/all_gather | solution.py:69
  8.6 250.1 %all-gather.11.cloned.1.call-start = ((), (), s32[]{:S(2)}) async-start(), calls=%async_computation.3 | async-start | bytes 6684672 | tf_op jit(solution)/shard_map/all_gather | solution.py:78
  191.9 280.2 %all-reduce.2.cloned.1.call-start = ((), (), s32[]{:S(2)}) async-start(), calls=%async_computation | async-start | bytes 8388608 | tf_op jit(solution)/shard_map/psum | solution.py:94
  258.8 3.4 copy-start.1
  262.3 9.3 %copy-start = (f32[12,64,128]{2,1,0:T(8,128)}, f32[12,64,128]{2,1,0:T(8,128)S(1)}, u32[]{:S(2)}) copy-start(f32[12,64,128]{2,1,0:T(8,128)S(1)} %subtract_select_fusion) | copy-start | bytes 1179652
Sparse Core Ops, SparseCore 0:
  9.8 75.5 all-gather.8
  87.2 97.3 all-gather.6
  192.0 66.7 all-gather.10
  271.7 200.2 all-reduce.1
